TPU v7x, 32 devices: a whole 2x2x4 slice. The times are simulated.
32 devices in a mesh: depth: 16 (over z, y, x), batch: 2 (over core).
Axes of the slice: x: 2, y: 2, z: 4, core: 2. Of those that a mesh axis runs over, the one named last changes fastest.
Arguments:
- inputs: float32 [4, 64, 512], P('batch'), parts along dimension 0, may hold values from -6 to 6
- attn_in: bfloat16 [16, 512, 1536], P('depth'), may hold values from -0.25 to 0.25
- attn_out: bfloat16 [16, 512, 512], P('depth'), may hold values from -0.25 to 0.25
- mlp_in: bfloat16 [16, 512, 1024], P('depth'), may hold values from -0.25 to 0.25
- mlp_out: bfloat16 [16, 1024, 512], P('depth'), may hold values from -0.1875 to 0.1875
- norm_gain: float32 [16, 512], P('depth'), may hold values from 0.25 to 1.75
- head_gain: float32 [16, 64], P('depth'), may hold values from 0.25 to 1.75
Outputs:
- states: float32 [16, 4, 64, 512], P('depth', 'batch'), parts along dimension 1
- coarse_points: float32 [16, 4, 64, 512], P('depth', 'batch'), parts along dimension 1
There are 2 independent parts, one for each index of `batch`. A program takes and returns all parts, laid end to end along the dimension named above; an argument that names none is the same for every part. Nothing has to cross between parts.
All inputs are finite; a program needn't handle non-finite values.
Results may differ from a plain program's by a relative error of at most 0.014.
Values sent between devices are 32-bit elements; how exact they have to be, the bound alone decides.
A program may use at most 64 MiB of HBM per device.

v0:
```python
import functools
import math

import jax
import jax.numpy as jnp
from jax import lax
from jax.experimental import pallas as pl
from jax.experimental.pallas import tpu as pltpu
from jax.sharding import PartitionSpec as P

COARSEN = 4
GROUP = 256
PIECES = 2
LAG = 3

step_size = 0.25
epsilon = 1e-06

FIRST, CHAIN, COARSE, RELAX, FINAL = range(5)
STAGES = 5
MESH = pl.DeviceIdType.MESH


def kernel(
    blocks, inputs, h_qkv, h_out, h_up, h_down, h_gain, h_head, states, coarse,
    w_qkv, w_out, w_up, w_down, in_gain, qk_gain, keys_ref, values_ref, load_sem, rx, tx, base, ends, term, share, parts, gathered, same_head, head_scale,
    send_sem, recv_sem, share_send, share_recv, ahead_send, own_send, own_recv, back_send,
):
    micro, frames, width = inputs.shape
    head_dim = qk_gain.shape[1]
    rows = frames // COARSEN
    device = lax.axis_index("depth")
    position = lax.rem(device, COARSEN)
    block = device // COARSEN
    has_next = block < blocks - 1
    last = COARSEN - 1
    is_last = position == last

    loads = [
        pltpu.make_async_copy(source, target, load_sem.at[i])
        for i, (source, target) in enumerate((
            (h_head, qk_gain), (h_gain, in_gain), (inputs, rx.at[FIRST]), (h_qkv, w_qkv),
            (h_up, w_up), (h_out, w_out), (h_down, w_down),
        ))
    ]
    for load in loads:
        load.start()

    def at(depth):
        return {"depth": depth}

    barrier = pltpu.get_barrier_semaphore()
    for i in range(COARSEN):
        @pl.when(block > 0)
        def _():
            pl.semaphore_signal(barrier, inc=1, device_id=at((block - 1) * COARSEN + i), device_id_type=MESH)

        @pl.when(has_next)
        def _():
            pl.semaphore_signal(barrier, inc=1, device_id=at((block + 1) * COARSEN + i), device_id_type=MESH)

    for i in range(1, COARSEN):
        other = block * COARSEN + lax.rem(position + i, COARSEN)
        pl.semaphore_signal(barrier, inc=1, device_id=at(other), device_id_type=MESH)

    heads_of = lax.broadcasted_iota(jnp.int32, (GROUP, GROUP), 0) // head_dim
    heads_at = lax.broadcasted_iota(jnp.int32, (GROUP, GROUP), 1) // head_dim
    same_head[...] = jnp.where(heads_of == heads_at, 1.0, 0.0).astype(jnp.bfloat16)
    keys_ref[...] = jnp.zeros_like(keys_ref)
    values_ref[...] = jnp.zeros_like(values_ref)
    loads[0].wait()
    head_scale[...] = jnp.concatenate([qk_gain[...]] * (width // head_dim), axis=1)

    neighbours = (block > 0).astype(jnp.int32) + has_next.astype(jnp.int32)
    pl.semaphore_wait(barrier, COARSEN - 1 + COARSEN * neighbours)

    for load in loads[1:]:
        load.wait()

    def delta(current, unit):
        piece = lax.rem(unit, PIECES)
        here = pl.ds(pl.multiple_of(piece * frames, frames), frames)
        square_mean = jnp.mean(current * current, axis=-1, keepdims=True)
        normed = (current * lax.rsqrt(square_mean + epsilon) * in_gain[...]).astype(jnp.bfloat16)
        projected = jnp.dot(normed, w_qkv[0], preferred_element_type=jnp.float32)
        same = same_head[...]
        copies = GROUP // head_dim
        causal = lax.broadcasted_iota(jnp.int32, (frames, GROUP), 0) + piece * frames >= lax.rem(
            lax.broadcasted_iota(jnp.int32, (frames, GROUP), 1), PIECES * frames
        )

        starts = range(0, width, GROUP)
        parts_of = [projected[:, start:start + GROUP] for start in range(0, 2 * width, GROUP)]
        squares = jnp.concatenate([(part * part).astype(jnp.bfloat16) for part in parts_of], axis=0)
        means = jnp.dot(squares, same, preferred_element_type=jnp.float32) * (1.0 / head_dim)
        scales = lax.rsqrt(means + epsilon)

        def head_norm(i, start):
            scale = scales[i * frames:(i + 1) * frames] * head_scale[:, start:start + GROUP]
            return (parts_of[i] * scale).astype(jnp.bfloat16)

        raised = jnp.dot(normed, w_up[0], preferred_element_type=jnp.float32)
        hidden = jax.nn.gelu(raised, approximate=True).astype(jnp.bfloat16)
        weights, mixes = [], []
        for i, start in enumerate(starts):
            query = head_norm(i, start)
            key = head_norm(i + len(starts), start)
            value = projected[:, 2 * width + start:2 * width + start + GROUP].astype(jnp.bfloat16)
            part = slice(start, start + GROUP)
            keys_ref[here, part] = key
            values_ref[here, part] = value
            keys = jnp.concatenate([keys_ref[:, part]] * copies, axis=0) * same
            values = jnp.concatenate([values_ref[:, part]] * copies, axis=0) * same
            scores = lax.dot_general(
                query, keys, (((1,), (1,)), ((), ())), preferred_element_type=jnp.float32
            ) * (1.0 / math.sqrt(head_dim))
            weight = jnp.where(causal, jnp.exp(scores), 0.0).astype(jnp.bfloat16)
            weights.append(weight)
            mixes.append(jnp.dot(weight, values, preferred_element_type=jnp.float32))
        totals = jnp.dot(jnp.concatenate(weights, axis=0), same, preferred_element_type=jnp.float32)
        contexts = [
            (mixed / totals[i * frames:(i + 1) * frames]).astype(jnp.bfloat16)
            for i, mixed in enumerate(mixes)
        ]
        context = jnp.concatenate(contexts, axis=1)
        return jnp.dot(context, w_out[0], preferred_element_type=jnp.float32) + jnp.dot(
            hidden, w_down[0], preferred_element_type=jnp.float32
        )

    def active(stage):
        return (
            (stage == FIRST)
            | ((stage == CHAIN) & (position > 0))
            | ((stage == COARSE) & (block > 0))
            | ((stage == RELAX) & (block > 0) & (position > 0))
            | ((stage == FINAL) & (block > 1) & (position < last))
        )

    def passes_on(stage):
        return (
            ((stage == FIRST) & (position == 0))
            | ((stage == CHAIN) & (position > 0) & (position < last))
            | ((stage == COARSE) & (block > 0) & (position == 0))
            | ((stage == RELAX) & (block > 0) & (position > 0) & ((position < last) | has_next))
            | ((stage == FINAL) & (block > 1) & (position < last - 1))
        )

    def is_state(stage):
        return (
            ((stage <= CHAIN) & (block == 0))
            | (((stage == COARSE) | (stage == RELAX)) & (block == 1))
            | ((stage == RELAX) & is_last)
            | (stage == FINAL)
        )

    def hop(stage, seq):
        target = jnp.where(
            stage <= CHAIN, CHAIN, jnp.where((stage == FINAL) | ((stage == RELAX) & is_last), FINAL, RELAX)
        )
        return pltpu.make_async_remote_copy(
            src_ref=tx.at[stage, seq], dst_ref=rx.at[target, seq],
            send_sem=send_sem.at[stage, seq], recv_sem=recv_sem.at[target, seq],
            device_id=at(device + 1), device_id_type=MESH,
        )

    def own_rows(of):
        return pl.ds(pl.multiple_of(of * rows, rows), rows)

    def give_share(seq, i):
        other = lax.rem(position + i, COARSEN)
        return pltpu.make_async_remote_copy(
            src_ref=term.at[seq, own_rows(other)], dst_ref=parts.at[seq, i - 1],
            send_sem=share_send.at[seq, i - 1], recv_sem=share_recv.at[seq],
            device_id=at(block * COARSEN + other), device_id_type=MESH,
        )

    def scatter_end(seq, i):
        return pltpu.make_async_remote_copy(
            src_ref=term.at[seq, own_rows(i)], dst_ref=parts.at[seq, 0],
            send_sem=share_send.at[seq, i], recv_sem=share_recv.at[seq],
            device_id=at(i), device_id_type=MESH,
        )

    def give_ahead(seq, i):
        other = lax.rem(position + i, COARSEN)
        return pltpu.make_async_remote_copy(
            src_ref=share.at[seq], dst_ref=rx.at[COARSE, seq, own_rows(position)],
            send_sem=ahead_send.at[seq, i], recv_sem=recv_sem.at[COARSE, seq],
            device_id=at((block + 1) * COARSEN + other), device_id_type=MESH,
        )

    def give_own(seq, i):
        other = lax.rem(position + i, COARSEN)
        return pltpu.make_async_remote_copy(
            src_ref=share.at[seq], dst_ref=gathered.at[seq, own_rows(position)],
            send_sem=own_send.at[seq, i - 1], recv_sem=own_recv.at[seq],
            device_id=at(block * COARSEN + other), device_id_type=MESH,
        )

    def landed(ref, sem):
        pltpu.make_async_copy(ref, ref, sem).wait()

    def give_back(seq):
        return pltpu.make_async_remote_copy(
            src_ref=rx.at[COARSE, seq], dst_ref=gathered.at[seq],
            send_sem=back_send.at[seq], recv_sem=own_recv.at[seq],
            device_id=at(device - COARSEN), device_id_type=MESH,
        )

    def finish(seq):
        mine = own_rows(position)

        @pl.when((block == 0) & is_last)
        def _():
            share[seq] = term[seq, mine]

        @pl.when((block == 0) & jnp.logical_not(is_last))
        def _():
            landed(parts.at[seq, 0], share_recv.at[seq])
            share[seq] = parts[seq, 0]

        @pl.when(block > 0)
        def _():
            landed(parts.at[seq], share_recv.at[seq])
            share[seq] = (term[seq, mine] + parts[seq, 0]) + (parts[seq, 1] + parts[seq, 2])

        @pl.when(has_next)
        def _():
            for i in range(COARSEN):
                give_ahead(seq, i).start()

        @pl.when(jnp.logical_not(has_next))
        def _():
            for i in range(1, COARSEN):
                give_own(seq, i).start()
            gathered[seq, mine] = share[seq]

    def turn(step, carry):
        stage, seq = step // micro, lax.rem(step, micro)

        @pl.when(active(stage))
        def _():
            @pl.when(stage > FIRST)
            def _():
                landed(rx.at[stage, seq], recv_sem.at[stage, seq])

            current = rx[stage, seq]
            change = step_size * delta(current, seq)
            moved = current + change

            @pl.when(passes_on(stage))
            def _():
                tx[stage, seq] = moved
                hop(stage, seq).start()

            @pl.when(stage == FIRST)
            def _():
                base[seq] = change

            @pl.when((stage == CHAIN) & is_last)
            def _():
                ends[seq] = moved - rx[FIRST, seq]

                @pl.when(block == 0)
                def _():
                    term[seq] = moved
                    for i in range(last):
                        scatter_end(seq, i).start()
                    finish(seq)

            @pl.when(stage == COARSE)
            def _():
                increment = change - base[seq]

                @pl.when(is_last)
                def _():
                    term[seq] = increment + (ends[seq] + current)

                @pl.when(jnp.logical_not(is_last))
                def _():
                    term[seq] = increment

                for i in range(1, COARSEN):
                    give_share(seq, i).start()
                give_back(seq).start()

                @pl.when(seq >= LAG)
                def _():
                    finish(seq - LAG)

            @pl.when(is_state(stage))
            def _():
                states[0, seq] = moved

        return carry

    lax.fori_loop(0, RELAX * micro, turn, 0)

    for seq in range(micro):
        early = (block == 0) & is_last
        if seq < micro - LAG:
            early = early | (block > 0)

        @pl.when(jnp.logical_not(early))
        def _():
            finish(seq)

    lax.fori_loop(RELAX * micro, STAGES * micro, turn, 0)

    for seq in range(micro):
        @pl.when(has_next)
        def _():
            landed(gathered.at[seq], own_recv.at[seq])

        @pl.when(jnp.logical_not(has_next))
        def _():
            landed(gathered.at[seq, pl.ds(0, last * rows)], own_recv.at[seq])

    coarse[0] = gathered[...]

    for seq in range(micro):
        for stage in range(STAGES):
            @pl.when(passes_on(stage))
            def _():
                hop(stage, seq).wait_send()

        @pl.when((block == 0) & is_last)
        def _():
            for i in range(last):
                scatter_end(seq, i).wait_send()

        @pl.when(block > 0)
        def _():
            for i in range(1, COARSEN):
                give_share(seq, i).wait_send()
            give_back(seq).wait_send()

        @pl.when(has_next)
        def _():
            for i in range(COARSEN):
                give_ahead(seq, i).wait_send()

        @pl.when(jnp.logical_not(has_next))
        def _():
            for i in range(1, COARSEN):
                give_own(seq, i).wait_send()


def solution(mesh):
    blocks = mesh.shape["depth"] // COARSEN

    def on_device(inputs, attn_in, attn_out, mlp_in, mlp_out, norm_gain, head_gain):
        whole = inputs.shape
        micro, frames, width = whole[0] * PIECES, whole[1] // PIECES, whole[2]
        rows = frames // COARSEN
        state = (micro, frames, width)
        out = jax.ShapeDtypeStruct((1,) + state, jnp.float32)
        vmem = pl.BlockSpec(memory_space=pltpu.VMEM)
        dma = pltpu.SemaphoreType.DMA
        weights = (attn_in, attn_out, mlp_in, mlp_out, norm_gain, head_gain)
        results = pl.pallas_call(
            functools.partial(kernel, blocks),
            out_shape=(out, out),
            in_specs=[pl.BlockSpec(memory_space=pl.ANY)] * 7,
            out_specs=(vmem, vmem),
            scratch_shapes=[
                *(pltpu.VMEM(weight.shape, weight.dtype) for weight in weights),
                pltpu.VMEM(whole[1:], jnp.bfloat16),
                pltpu.VMEM(whole[1:], jnp.bfloat16),
                dma((len(weights) + 1,)),
                pltpu.VMEM((STAGES,) + state, jnp.float32),
                pltpu.VMEM((STAGES,) + state, jnp.float32),
                pltpu.VMEM(state, jnp.float32),
                pltpu.VMEM(state, jnp.float32),
                pltpu.VMEM(state, jnp.float32),
                pltpu.VMEM((micro, rows, width), jnp.float32),
                pltpu.VMEM((micro, COARSEN - 1, rows, width), jnp.float32),
                pltpu.VMEM(state, jnp.float32),
                pltpu.VMEM((GROUP, GROUP), jnp.bfloat16),
                pltpu.VMEM((1, width), jnp.float32),
                dma((STAGES, micro)),
                dma((STAGES, micro)),
                dma((micro, COARSEN - 1)),
                dma((micro,)),
                dma((micro, COARSEN)),
                dma((micro, COARSEN - 1)),
                dma((micro,)),
                dma((micro,)),
            ],
            compiler_params=pltpu.CompilerParams(
                collective_id=0, has_side_effects=True, vmem_limit_bytes=64_000_000
            ),
        )(inputs.reshape(state), *weights)
        return tuple(result.reshape((1,) + whole) for result in results)

    in_specs = (
        P("batch", None, None),
        P("depth", None, None),
        P("depth", None, None),
        P("depth", None, None),
        P("depth", None, None),
        P("depth", None),
        P("depth", None),
    )
    out_specs = (P("depth", "batch", None, None), P("depth", "batch", None, None))
    return jax.shard_map(
        on_device, mesh=mesh, in_specs=in_specs, out_specs=out_specs, check_vma=False
    )
```

profile of v0, /device:TPU:28, one launch (start us, length us, event | category | flops | bytes accessed | tf_op | source)
XLA Modules:
  0.0 80.5 jit_solution(5707204759917204512)
XLA Ops:
  0.6 76.5 %shard_map.86 = (f32[1,4,32,512]{3,2,1,0:T(8,128)}, f32[1,4,32,512]{3,2,1,0:T(8,128)}) custom-call(f32[4,32,512]{2,1,0:T(8,128)} %bitcast.3, bf16[1,512,1536]{2,1,0:T(8,128)(2,1)} %h_qkv.1, bf16[1,512,512]{2,1,0:T(8,128)(2,1)} %h_out.1, bf16[1,512,1024]{2,1,0:T(8,128)(2,1)} %h_up.1, bf16[1,1024,512]{2,1,0:T(8,128)(2,1)} %h_down.1, f32[1,512]{1,0:T(1,128)} %h_gain.1, ...), custom_call_target="tpu_custom_call" | custom-call | tf_op jit(solution)/shard_map/pallas_call | solution.py:361
  77.1 1.7 %copy.11 = f32[1,2,64,512]{3,2,1,0:T(8,128)} copy(f32[1,2,64,512]{3,2,1,0:T(8,128)} %bitcast.5) | data formatting | bytes 524288
  78.8 1.7 %copy.12 = f32[1,2,64,512]{3,2,1,0:T(8,128)} copy(f32[1,2,64,512]{3,2,1,0:T(8,128)} %bitcast.4) | data formatting | bytes 524288
where the time goes:
time: 80.7 us; the launch traced here: 80.5 us
  Pallas kernels  76.5 us (95%)
  local copies, waits for them, and re-layouts  3.34 us (4%)
    pallas_call x1, Pallas kernels, on_device(): pl.pallas_call(functools.partial(kernel, blocks), out_shape=(out, out), i...  76.5 us
    unnamed x2, local copies, waits for them, and re-layouts  3.34 us

commit v1 on v0

--- a/solution.py
+++ b/solution.py
@@ -11,7 +11,7 @@
 COARSEN = 4
 GROUP = 256
 PIECES = 2
-LAG = 3
+LAG = 2
 
 step_size = 0.25
 epsilon = 1e-06
@@ -23,7 +23,7 @@
 
 def kernel(
     blocks, inputs, h_qkv, h_out, h_up, h_down, h_gain, h_head, states, coarse,
-    w_qkv, w_out, w_up, w_down, in_gain, qk_gain, keys_ref, values_ref, load_sem, rx, tx, base, ends, term, share, parts, gathered, same_head, head_scale,
+    w_qkv, w_out, w_up, w_down, in_gain, qk_gain, keys_ref, values_ref, load_sem, rx, tx, base, ends, term, share, parts, gathered, same_head, head_scale, query_scale,
     send_sem, recv_sem, share_send, share_recv, ahead_send, own_send, own_recv, back_send,
 ):
     micro, frames, width = inputs.shape
@@ -70,6 +70,7 @@
     values_ref[...] = jnp.zeros_like(values_ref)
     loads[0].wait()
     head_scale[...] = jnp.concatenate([qk_gain[...]] * (width // head_dim), axis=1)
+    query_scale[...] = head_scale[...] * (1.0 / math.sqrt(head_dim))
 
     neighbours = (block > 0).astype(jnp.int32) + has_next.astype(jnp.int32)
     pl.semaphore_wait(barrier, COARSEN - 1 + COARSEN * neighbours)
@@ -80,56 +81,72 @@
     def delta(current, unit):
         piece = lax.rem(unit, PIECES)
         here = pl.ds(pl.multiple_of(piece * frames, frames), frames)
-        square_mean = jnp.mean(current * current, axis=-1, keepdims=True)
-        normed = (current * lax.rsqrt(square_mean + epsilon) * in_gain[...]).astype(jnp.bfloat16)
-        projected = jnp.dot(normed, w_qkv[0], preferred_element_type=jnp.float32)
+        spread = jnp.mean(current * current, axis=-1, keepdims=True) + epsilon
+        row_scale = lax.rsqrt(spread)
+        gained = (current * in_gain[...]).astype(jnp.bfloat16)
         same = same_head[...]
         copies = GROUP // head_dim
         causal = lax.broadcasted_iota(jnp.int32, (frames, GROUP), 0) + piece * frames >= lax.rem(
             lax.broadcasted_iota(jnp.int32, (frames, GROUP), 1), PIECES * frames
         )
-
         starts = range(0, width, GROUP)
-        parts_of = [projected[:, start:start + GROUP] for start in range(0, 2 * width, GROUP)]
-        squares = jnp.concatenate([(part * part).astype(jnp.bfloat16) for part in parts_of], axis=0)
-        means = jnp.dot(squares, same, preferred_element_type=jnp.float32) * (1.0 / head_dim)
-        scales = lax.rsqrt(means + epsilon)
-
-        def head_norm(i, start):
-            scale = scales[i * frames:(i + 1) * frames] * head_scale[:, start:start + GROUP]
-            return (parts_of[i] * scale).astype(jnp.bfloat16)
-
-        raised = jnp.dot(normed, w_up[0], preferred_element_type=jnp.float32)
-        hidden = jax.nn.gelu(raised, approximate=True).astype(jnp.bfloat16)
+        half = w_up.shape[2] // 2
+
+        def project(part):
+            return jnp.dot(
+                gained, w_qkv[0, :, part * width:(part + 1) * width], preferred_element_type=jnp.float32
+            )
+
+        def head_norm(rows_of, scale_of):
+            cut = [rows_of[:, start:start + GROUP] for start in starts]
+            squares = jnp.concatenate([(part * part).astype(jnp.bfloat16) for part in cut], axis=0)
+            means = jnp.dot(squares, same, preferred_element_type=jnp.float32) * (1.0 / head_dim)
+            scales = lax.rsqrt(means + jnp.concatenate([epsilon * spread] * len(cut), axis=0))
+            return [
+                (part * (scales[i * frames:(i + 1) * frames] * scale_of[:, start:start + GROUP])).astype(jnp.bfloat16)
+                for i, (part, start) in enumerate(zip(cut, starts))
+            ]
+
+        def raise_half(i):
+            raised = jnp.dot(gained, w_up[0, :, i * half:(i + 1) * half], preferred_element_type=jnp.float32)
+            return jax.nn.gelu(raised * row_scale, approximate=True).astype(jnp.bfloat16)
+
+        def lower_half(i, hidden):
+            return jnp.dot(hidden, w_down[0, i * half:(i + 1) * half], preferred_element_type=jnp.float32)
+
+        key_rows = project(1)
+        query_rows = project(0)
+        keys_of = head_norm(key_rows, head_scale)
+        queries_of = head_norm(query_rows, query_scale)
+        values_of = (project(2) * row_scale).astype(jnp.bfloat16)
+        hidden = raise_half(0)
         weights, mixes = [], []
         for i, start in enumerate(starts):
-            query = head_norm(i, start)
-            key = head_norm(i + len(starts), start)
-            value = projected[:, 2 * width + start:2 * width + start + GROUP].astype(jnp.bfloat16)
             part = slice(start, start + GROUP)
-            keys_ref[here, part] = key
-            values_ref[here, part] = value
+            keys_ref[here, part] = keys_of[i]
+            values_ref[here, part] = values_of[:, part]
             keys = jnp.concatenate([keys_ref[:, part]] * copies, axis=0) * same
-            values = jnp.concatenate([values_ref[:, part]] * copies, axis=0) * same
             scores = lax.dot_general(
-                query, keys, (((1,), (1,)), ((), ())), preferred_element_type=jnp.float32
-            ) * (1.0 / math.sqrt(head_dim))
-            weight = jnp.where(causal, jnp.exp(scores), 0.0).astype(jnp.bfloat16)
-            weights.append(weight)
+                queries_of[i], keys, (((1,), (1,)), ((), ())), preferred_element_type=jnp.float32
+            )
+            weights.append(jnp.where(causal, jnp.exp(scores), 0.0).astype(jnp.bfloat16))
+        late = raise_half(1)
+        lowered = lower_half(0, hidden)
+        for weight, start in zip(weights, starts):
+            values = jnp.concatenate([values_ref[:, start:start + GROUP]] * copies, axis=0) * same
             mixes.append(jnp.dot(weight, values, preferred_element_type=jnp.float32))
         totals = jnp.dot(jnp.concatenate(weights, axis=0), same, preferred_element_type=jnp.float32)
+        lowered = lowered + lower_half(1, late)
         contexts = [
             (mixed / totals[i * frames:(i + 1) * frames]).astype(jnp.bfloat16)
             for i, mixed in enumerate(mixes)
         ]
         context = jnp.concatenate(contexts, axis=1)
-        return jnp.dot(context, w_out[0], preferred_element_type=jnp.float32) + jnp.dot(
-            hidden, w_down[0], preferred_element_type=jnp.float32
-        )
+        return jnp.dot(context, w_out[0], preferred_element_type=jnp.float32) + lowered
 
     def active(stage):
         return (
-            (stage == FIRST)
+            ((stage == FIRST) & ((block > 0) | (position == 0)))
             | ((stage == CHAIN) & (position > 0))
             | ((stage == COARSE) & (block > 0))
             | ((stage == RELAX) & (block > 0) & (position > 0))
@@ -378,6 +395,7 @@
                 pltpu.VMEM(state, jnp.float32),
                 pltpu.VMEM((GROUP, GROUP), jnp.bfloat16),
                 pltpu.VMEM((1, width), jnp.float32),
+                pltpu.VMEM((1, width), jnp.float32),
                 dma((STAGES, micro)),
                 dma((STAGES, micro)),
                 dma((micro, COARSEN - 1)),

time: 80.7 us -> 78.2 us (0.969)
  Pallas kernels: 76.5 us -> 74.1 us
    pallas_call x1, Pallas kernels: 76.5 us -> 74.1 us  [on_device(): pl.pallas_call(functools.partial(kernel, blocks), out_shape=(out, out), i...]
where the time goes in v1:
time: 78.2 us; the launch traced here: 78.1 us
  Pallas kernels  74.1 us (95%)
  local copies, waits for them, and re-layouts  3.34 us (4%)
    pallas_call x1, Pallas kernels, on_device(): pl.pallas_call(functools.partial(kernel, blocks), out_shape=(out, out), i...  74.1 us
    unnamed x2, local copies, waits for them, and re-layouts  3.34 us

profile of v1, /device:TPU:28, one launch (start us, length us, event | category | flops | bytes accessed | tf_op | source)
XLA Modules:
  0.0 78.1 jit_solution(5943556522963153737)
XLA Ops:
  0.6 74.1 %shard_map.86 = (f32[1,4,32,512]{3,2,1,0:T(8,128)}, f32[1,4,32,512]{3,2,1,0:T(8,128)}) custom-call(f32[4,32,512]{2,1,0:T(8,128)} %bitcast.3, bf16[1,512,1536]{2,1,0:T(8,128)(2,1)} %h_qkv.1, bf16[1,512,512]{2,1,0:T(8,128)(2,1)} %h_out.1, bf16[1,512,1024]{2,1,0:T(8,128)(2,1)} %h_up.1, bf16[1,1024,512]{2,1,0:T(8,128)(2,1)} %h_down.1, f32[1,512]{1,0:T(1,128)} %h_gain.1, ...), custom_call_target="tpu_custom_call" | custom-call | tf_op jit(solution)/shard_map/pallas_call | solution.py:378
  74.7 1.7 %copy.11 = f32[1,2,64,512]{3,2,1,0:T(8,128)} copy(f32[1,2,64,512]{3,2,1,0:T(8,128)} %bitcast.5) | data formatting | bytes 524288
  76.4 1.7 %copy.12 = f32[1,2,64,512]{3,2,1,0:T(8,128)} copy(f32[1,2,64,512]{3,2,1,0:T(8,128)} %bitcast.4) | data formatting | bytes 524288

commit v2 on v1

--- a/solution.py
+++ b/solution.py
@@ -11,7 +11,7 @@
 COARSEN = 4
 GROUP = 256
 PIECES = 2
-LAG = 2
+LAG = 3
 
 step_size = 0.25
 epsilon = 1e-06
@@ -301,27 +301,28 @@
                     give_share(seq, i).start()
                 give_back(seq).start()
 
-                @pl.when(seq >= LAG)
-                def _():
-                    finish(seq - LAG)
-
             @pl.when(is_state(stage))
             def _():
                 states[0, seq] = moved
 
+            since = step - COARSE * micro - LAG
+            turns = jnp.where(position == 1, micro, micro - LAG)
+
+            @pl.when((block > 0) & (since >= 0) & (since < turns))
+            def _():
+                finish(since)
+
         return carry
 
+    def finish_left(first, last_seq, when):
+        for seq in range(first, last_seq):
+            @pl.when(when)
+            def _():
+                finish(seq)
+
     lax.fori_loop(0, RELAX * micro, turn, 0)
-
-    for seq in range(micro):
-        early = (block == 0) & is_last
-        if seq < micro - LAG:
-            early = early | (block > 0)
-
-        @pl.when(jnp.logical_not(early))
-        def _():
-            finish(seq)
-
+    finish_left(0, micro, (block == 0) & jnp.logical_not(is_last))
+    finish_left(max(micro - LAG, 0), micro, (block > 0) & (position != 1))
     lax.fori_loop(RELAX * micro, STAGES * micro, turn, 0)
 
     for seq in range(micro):
@@ -406,7 +407,7 @@
                 dma((micro,)),
             ],
             compiler_params=pltpu.CompilerParams(
-                collective_id=0, has_side_effects=True, vmem_limit_bytes=64_000_000
+                collective_id=0, has_side_effects=True, vmem_limit_bytes=56_000_000
             ),
         )(inputs.reshape(state), *weights)
         return tuple(result.reshape((1,) + whole) for result in results)

time: 78.2 us -> 73.2 us (0.936)
  Pallas kernels: 74.1 us -> 69.6 us
    pallas_call x1, Pallas kernels: 74.1 us -> 69.6 us  [on_device(): pl.pallas_call(functools.partial(kernel, blocks), out_shape=(out, out), i...]
    unnamed x2 -> x6, local copies, waits for them, and re-layouts: 3.34 us -> 2.74 us
where the time goes in v2:
time: 73.2 us; the launch traced here: 73 us
  Pallas kernels  69.6 us (95%)
  local copies, waits for them, and re-layouts  2.74 us (4%)
    pallas_call x1, Pallas kernels, on_device(): pl.pallas_call(functools.partial(kernel, blocks), out_shape=(out, out), i...  69.6 us
    unnamed x6, local copies, waits for them, and re-layouts  2.74 us

profile of v2, /device:TPU:28, one launch (start us, length us, event | category | flops | bytes accessed | tf_op | source)
XLA Modules:
  0.0 73.0 jit_solution(9396036565741735618)
XLA Ops:
  0.6 0.0 copy-start
  0.6 0.7 copy-done
  1.3 0.0 copy-start.1
  1.3 0.7 copy-done.1
  2.0 69.6 %shard_map.86 = (f32[1,4,32,512]{3,2,1,0:T(8,128)S(1)}, f32[1,4,32,512]{3,2,1,0:T(8,128)S(1)}) custom-call(f32[4,32,512]{2,1,0:T(8,128)} %bitcast.5, bf16[1,512,1536]{2,1,0:T(8,128)(2,1)} %h_qkv.1, bf16[1,512,512]{2,1,0:T(8,128)(2,1)} %h_out.1, bf16[1,512,1024]{2,1,0:T(8,128)(2,1)} %h_up.1, bf16[1,1024,512]{2,1,0:T(8,128)(2,1)} %h_down.1, ...), custom_call_target="tpu_custom_call" | custom-call | tf_op jit(solution)/shard_map/pallas_call | solution.py:379
  71.6 0.7 copy.11
  72.3 0.7 copy.12
Async XLA Ops:
  0.6 0.7 copy-start
  1.3 0.7 copy-start.1

commit v3 on v2

--- a/solution.py
+++ b/solution.py
@@ -36,13 +36,18 @@
     last = COARSEN - 1
     is_last = position == last
 
+    def columns(ref, part):
+        return ref.at[0, :, pl.ds(part * width, width)]
+
     loads = [
         pltpu.make_async_copy(source, target, load_sem.at[i])
         for i, (source, target) in enumerate((
-            (h_head, qk_gain), (h_gain, in_gain), (inputs, rx.at[FIRST]), (h_qkv, w_qkv),
-            (h_up, w_up), (h_out, w_out), (h_down, w_down),
+            (h_head, qk_gain), (h_gain, in_gain), (inputs, rx.at[FIRST]),
+            *((columns(h_qkv, part), columns(w_qkv, part)) for part in (1, 0, 2)),
+            (h_up, w_up), (h_down, w_down), (h_out, w_out),
         ))
     ]
+    load_keys, load_queries, load_values, load_up, load_down, load_out = loads[3:]
     for load in loads:
         load.start()
 
@@ -73,12 +78,17 @@
     query_scale[...] = head_scale[...] * (1.0 / math.sqrt(head_dim))
 
     neighbours = (block > 0).astype(jnp.int32) + has_next.astype(jnp.int32)
-    pl.semaphore_wait(barrier, COARSEN - 1 + COARSEN * neighbours)
-
-    for load in loads[1:]:
+    loads[1].wait()
+    loads[2].wait()
+
+    def keep(value, load):
+        return value
+
+    def fetched(value, load):
         load.wait()
-
-    def delta(current, unit):
+        return value
+
+    def delta(current, unit, after=keep):
         piece = lax.rem(unit, PIECES)
         here = pl.ds(pl.multiple_of(piece * frames, frames), frames)
         spread = jnp.mean(current * current, axis=-1, keepdims=True) + epsilon
@@ -92,9 +102,9 @@
         starts = range(0, width, GROUP)
         half = w_up.shape[2] // 2
 
-        def project(part):
+        def project(part, load):
             return jnp.dot(
-                gained, w_qkv[0, :, part * width:(part + 1) * width], preferred_element_type=jnp.float32
+                after(gained, load), w_qkv[0, :, part * width:(part + 1) * width], preferred_element_type=jnp.float32
             )
 
         def head_norm(rows_of, scale_of):
@@ -114,11 +124,12 @@
         def lower_half(i, hidden):
             return jnp.dot(hidden, w_down[0, i * half:(i + 1) * half], preferred_element_type=jnp.float32)
 
-        key_rows = project(1)
-        query_rows = project(0)
+        key_rows = project(1, load_keys)
+        query_rows = project(0, load_queries)
         keys_of = head_norm(key_rows, head_scale)
         queries_of = head_norm(query_rows, query_scale)
-        values_of = (project(2) * row_scale).astype(jnp.bfloat16)
+        values_of = (project(2, load_values) * row_scale).astype(jnp.bfloat16)
+        after(gained, load_up)
         hidden = raise_half(0)
         weights, mixes = [], []
         for i, start in enumerate(starts):
@@ -131,6 +142,7 @@
             )
             weights.append(jnp.where(causal, jnp.exp(scores), 0.0).astype(jnp.bfloat16))
         late = raise_half(1)
+        after(hidden, load_down)
         lowered = lower_half(0, hidden)
         for weight, start in zip(weights, starts):
             values = jnp.concatenate([values_ref[:, start:start + GROUP]] * copies, axis=0) * same
@@ -142,6 +154,7 @@
             for i, mixed in enumerate(mixes)
         ]
         context = jnp.concatenate(contexts, axis=1)
+        after(context, load_out)
         return jnp.dot(context, w_out[0], preferred_element_type=jnp.float32) + lowered
 
     def active(stage):
@@ -320,7 +333,22 @@
             def _():
                 finish(seq)
 
-    lax.fori_loop(0, RELAX * micro, turn, 0)
+    current = rx[FIRST, 0]
+    change = step_size * delta(current, 0, fetched)
+    base[0] = change
+    pl.semaphore_wait(barrier, COARSEN - 1 + COARSEN * neighbours)
+    moved = current + change
+
+    @pl.when(position == 0)
+    def _():
+        tx[FIRST, 0] = moved
+        hop(FIRST, 0).start()
+
+    @pl.when(block == 0)
+    def _():
+        states[0, 0] = moved
+
+    lax.fori_loop(1, RELAX * micro, turn, 0)
     finish_left(0, micro, (block == 0) & jnp.logical_not(is_last))
     finish_left(max(micro - LAG, 0), micro, (block > 0) & (position != 1))
     lax.fori_loop(RELAX * micro, STAGES * micro, turn, 0)
@@ -362,6 +390,17 @@
         def _():
             for i in range(1, COARSEN):
                 give_own(seq, i).wait_send()
+
+
+def hand_over(states, coarse, states_out, coarse_out, sem):
+    copies = [
+        pltpu.make_async_copy(source, target, sem.at[i])
+        for i, (source, target) in enumerate(((states, states_out), (coarse, coarse_out)))
+    ]
+    for copy in copies:
+        copy.start()
+    for copy in copies:
+        copy.wait()
 
 
 def solution(mesh):
@@ -385,7 +424,7 @@
                 *(pltpu.VMEM(weight.shape, weight.dtype) for weight in weights),
                 pltpu.VMEM(whole[1:], jnp.bfloat16),
                 pltpu.VMEM(whole[1:], jnp.bfloat16),
-                dma((len(weights) + 1,)),
+                dma((len(weights) + 3,)),
                 pltpu.VMEM((STAGES,) + state, jnp.float32),
                 pltpu.VMEM((STAGES,) + state, jnp.float32),
                 pltpu.VMEM(state, jnp.float32),
@@ -409,8 +448,15 @@
             compiler_params=pltpu.CompilerParams(
                 collective_id=0, has_side_effects=True, vmem_limit_bytes=56_000_000
             ),
-        )(inputs.reshape(state), *weights)
-        return tuple(result.reshape((1,) + whole) for result in results)
+        )(*(pltpu.with_memory_space_constraint(v, pltpu.HBM) for v in (inputs.reshape(state), *weights)))
+        return pl.pallas_call(
+            hand_over,
+            out_shape=(jax.ShapeDtypeStruct((1,) + whole, jnp.float32),) * 2,
+            in_specs=[pl.BlockSpec(memory_space=pl.ANY)] * 2,
+            out_specs=(pl.BlockSpec(memory_space=pltpu.HBM),) * 2,
+            scratch_shapes=[dma((2,))],
+            compiler_params=pltpu.CompilerParams(vmem_limit_bytes=1_000_000),
+        )(*(result.reshape((1,) + whole) for result in results))
 
     in_specs = (
         P("batch", None, None),

time: 73.2 us -> 69.9 us (0.955)
  local copies, waits for them, and re-layouts: 2.74 us -> 0 us
    unnamed x6 -> x0, local copies, waits for them, and re-layouts: 2.74 us -> none
    pallas_call x1, Pallas kernels: 69.6 us -> 68.3 us  [on_device(): pl.pallas_call(functools.partial(kernel, blocks), out_shape=(out, out), i...]
    pallas_call x0 -> x1, Pallas kernels: none -> 0.81 us  [on_device(): pl.pallas_call(hand_over, out_shape=(jax.ShapeDtypeStruct((1,) + whole, j...]
where the time goes in v3:
time: 69.9 us; the launch traced here: 69.7 us
  Pallas kernels  69.1 us (99%)
    pallas_call x1, Pallas kernels, on_device(): pl.pallas_call(functools.partial(kernel, blocks), out_shape=(out, out), i...  68.3 us

profile of v3, /device:TPU:28, one launch (start us, length us, event | category | flops | bytes accessed | tf_op | source)
XLA Modules:
  0.0 69.7 jit_solution(7415997131980841095)
XLA Ops:
  0.6 68.3 %shard_map.86 = (f32[1,4,32,512]{3,2,1,0:T(8,128)S(1)}, f32[1,4,32,512]{3,2,1,0:T(8,128)S(1)}) custom-call(f32[4,32,512]{2,1,0:T(8,128)} %bitcast.5, bf16[1,512,1536]{2,1,0:T(8,128)(2,1)} %h_qkv.1, bf16[1,512,512]{2,1,0:T(8,128)(2,1)} %h_out.1, bf16[1,512,1024]{2,1,0:T(8,128)(2,1)} %h_up.1, bf16[1,1024,512]{2,1,0:T(8,128)(2,1)} %h_down.1, f32[1,512]{1,0:T(1,128)} %h_gain.1, ...), custom_call_target="tpu_custom_call" | custom-call | tf_op jit(solution)/shard_map/pallas_call | solution.py:418
  68.9 0.8 %shard_map.87 = (f32[1,2,64,512]{3,2,1,0:T(8,128)}, f32[1,2,64,512]{3,2,1,0:T(8,128)}) custom-call(f32[1,2,64,512]{3,2,1,0:T(8,128)S(1)} %bitcast.3, f32[1,2,64,512]{3,2,1,0:T(8,128)S(1)} %bitcast.4), custom_call_target="tpu_custom_call" | custom-call | tf_op jit(solution)/shard_map/pallas_call | solution.py:452
